TPU v7x, 128 devices: a whole 4x4x4 slice. The times are simulated.
128 devices in a mesh: shards: 16 (over x, y), tensor: 4 (over z), section: 2 (over core).
Axes of the slice: x: 4, y: 4, z: 4, core: 2. Of those that a mesh axis runs over, the one named last changes fastest.
Arguments:
- gradient: bfloat16 [4, 768, 2048], P('section', 'tensor', 'shards'), may hold values from -36 to 36, as said below
- weight: bfloat16 [4, 768, 2048], P('section', 'tensor', 'shards'), may hold values from -0.21875 to 0.21875
- projector: float32 [4, 768, 256], P('section', 'tensor'), may hold values from -0.21875 to 0.21875
- first_moment: float32 [4, 256, 2048], P('section', 'tensor', 'shards'), may hold values from -0.3125 to 0.3125
- squared_moment: float32 [4, 256, 2048], P('section', 'tensor', 'shards'), may hold values from 1e-07 to 1e-05
- step_count: int32 [4], P('section'), may hold values from 1 to 11
- norm_gains: float32 [4, 768], P('section', 'tensor'), may hold values from 0.5 to 1.5
- gain_gradient: float32 [4, 768], P('section', 'tensor'), may hold values from -0.15625 to 0.15625
- gain_first: float32 [4, 768], P('section', 'tensor'), may hold values from -0.046875 to 0.046875
- gain_second: float32 [4, 768], P('section', 'tensor'), may hold values from 1e-08 to 1e-06
Outputs:
- weight_next: bfloat16 [4, 768, 2048], P('section', 'tensor', 'shards')
- fresh_projector: float32 [4, 768, 256], P('section', 'tensor')
- new_first: float32 [4, 256, 2048], P('section', 'tensor', 'shards')
- new_second: float32 [4, 256, 2048], P('section', 'tensor', 'shards')
- new_gains: float32 [4, 768], P('section', 'tensor')
- new_gain_first: float32 [4, 768], P('section', 'tensor')
- new_gain_second: float32 [4, 768], P('section', 'tensor')
Inputs may be any that keep to these rules, and one draw needn't show every extreme that they name: `gradient`: gradient entries are finite real numbers.
All inputs are finite; a program needn't handle non-finite values.
Results may differ from a plain program's by a relative error of at most 0.001.
Values sent between devices are 32-bit elements; how exact they have to be, the bound alone decides.
No kernel may reach another device: no remote copies, remote signals or barrier semaphores. Data moves between devices by JAX's collectives and lax.ppermute only.
A program may use at most 64 MiB of HBM per device.

v0:
```python
import jax
import jax.numpy as jnp
from jax import lax
from jax.sharding import PartitionSpec as P

NS_STEPS = 5
BETA_ONE = 0.9
BETA_TWO = 0.999
EPSILON = 1e-08
NORM_EPS = 1e-06
LEARN_RATE = 0.01
GALORE_SCALE = 0.25
WEIGHT_DECAY = 0.1


def newton_step(current, gram_matrix):
    return 1.5 * current - 0.5 * jnp.einsum(
        "mdr,mrs->mds", current, gram_matrix, precision=lax.Precision.HIGHEST
    )


def spread_orthogonalize(ranged):
    precision_highest = lax.Precision.HIGHEST
    squares = lax.psum(jnp.sum(ranged * ranged, axis=(1, 2)), ("shards", "tensor"))
    current = ranged / (jnp.sqrt(squares) + NORM_EPS)[:, None, None]
    for sweep_index in range(NS_STEPS):
        gram_matrix = lax.psum(
            jnp.einsum("mdr,mds->mrs", current, current, precision=precision_highest),
            ("shards", "tensor"),
        )
        current = newton_step(current, gram_matrix)
    return current


def shards(
    gradient,
    weight,
    projector,
    first_moment,
    squared_moment,
    step_count,
    norm_gains,
    gain_gradient,
    gain_first,
    gain_second,
):
    precision_highest = lax.Precision.HIGHEST
    gradient_widened = gradient.astype(jnp.float32)
    folded = lax.psum(
        jnp.einsum("mdf,mdr->mfr", gradient_widened, projector, precision=precision_highest),
        "tensor",
    )
    ranged_part = jnp.einsum("mdf,mfr->mdr", gradient_widened, folded, precision=precision_highest)
    ranged = lax.psum_scatter(ranged_part, "shards", scatter_dimension=1, tiled=True)
    fresh_projector = lax.all_gather(spread_orthogonalize(ranged), "shards", axis=1, tiled=True)
    projected_slice = jnp.einsum(
        "uqk,uqc->ukc", fresh_projector, gradient_widened, precision=precision_highest
    )
    own_rank = first_moment.shape[1]
    complete_rows = lax.psum(projected_slice, "tensor")
    projected = lax.dynamic_slice_in_dim(
        complete_rows, lax.axis_index("tensor") * own_rank, own_rank, 1
    )
    steps_float = step_count.astype(jnp.float32)[:, None, None]
    new_first = BETA_ONE * first_moment + (1.0 - BETA_ONE) * projected
    new_second = BETA_TWO * squared_moment + (1.0 - BETA_TWO) * projected * projected
    direction = (
        new_first
        / (1.0 - BETA_ONE**steps_float)
        / (jnp.sqrt(new_second / (1.0 - BETA_TWO**steps_float)) + EPSILON)
    )
    update = jnp.einsum(
        "hxp,hpq->hxq",
        fresh_projector,
        lax.all_gather(direction, "tensor", axis=1, tiled=True),
        precision=precision_highest,
    )
    weight_float = weight.astype(jnp.float32)
    weight_next = (
        weight_float - LEARN_RATE * (GALORE_SCALE * update + WEIGHT_DECAY * weight_float)
    ).astype(jnp.bfloat16)
    gain_steps = step_count.astype(jnp.float32)[:, None]
    new_gain_first = BETA_ONE * gain_first + (1.0 - BETA_ONE) * gain_gradient
    new_gain_second = BETA_TWO * gain_second + (1.0 - BETA_TWO) * gain_gradient * gain_gradient
    new_gains = norm_gains - LEARN_RATE * (new_gain_first / (1.0 - BETA_ONE**gain_steps)) / (
        jnp.sqrt(new_gain_second / (1.0 - BETA_TWO**gain_steps)) + EPSILON
    )
    return (
        weight_next,
        fresh_projector,
        new_first,
        new_second,
        new_gains,
        new_gain_first,
        new_gain_second,
    )


def solution(mesh):
    return jax.shard_map(
        shards,
        mesh=mesh,
        in_specs=(
            P("section", "tensor", "shards"),
            P("section", "tensor", "shards"),
            P("section", "tensor", None),
            P("section", "tensor", "shards"),
            P("section", "tensor", "shards"),
            P("section"),
            P("section", "tensor"),
            P("section", "tensor"),
            P("section", "tensor"),
            P("section", "tensor"),
        ),
        out_specs=(
            P("section", "tensor", "shards"),
            P("section", "tensor", None),
            P("section", "tensor", "shards"),
            P("section", "tensor", "shards"),
            P("section", "tensor"),
            P("section", "tensor"),
            P("section", "tensor"),
        ),
        check_vma=False,
    )
```

profile of v0, /device:TPU:0, one launch (start us, length us, event | category | flops | bytes accessed | tf_op | source)
XLA Modules:
  0.0 1052.9 jit_solution(11684637184179411351)
XLA Ops:
  7.2 0.0 copy-start
  7.2 0.0 all-reduce.10.cloned.1.call-start
  7.2 0.9 copy-done
  8.2 1.9 fusion.14
  10.1 0.0 copy-start.2
  10.1 0.0 all-reduce.10.cloned.1.call-update
  10.1 0.0 all-reduce.24.cloned.1.call-start
  10.2 45.4 %all-reduce.10.cloned.1.call-done = f32[2,128,256]{2,1,0:T(8,128)} async-done(((f32[2,128,256]{2,1,0:T(8,128)}), f32[2,128,256]{2,1,0:T(8,128)}) %all-reduce.10.cloned.1.call-update) | async-done | bytes 262160 | tf_op jit(solution)/shard_map/psum | solution.py:49
  55.5 0.0 copy-done.2
  55.6 1.3 convolution_bitcast_fusion
  56.8 1.1 copy.17
  57.9 0.0 all-reduce.24.cloned.1.call-update
  57.9 0.0 all-reduce.12.cloned.1.call-start
  58.0 0.0 copy-start.11
  58.0 0.6 copy-done.11
  58.6 0.6 dynamic-slice
  59.9 84.4 %all-reduce.24.cloned.1.call-done = f32[2,192,256]{2,0,1:T(2,128)} async-done(((f32[2,192,256]{2,0,1:T(2,128)}), f32[2,192,256]{2,0,1:T(2,128)}) %all-reduce.24.cloned.1.call-update) | async-done | bytes 393232
  144.2 0.9 multiply_reduce_fusion
  145.1 176.9 %psum.57 = f32[2]{0:T(128)S(1)} all-reduce(f32[2]{0:T(128)S(1)} %get-tuple-element.20), channel_id=1, replica_groups=mesh['shards'=16,'tensor'=4,'section'=2] {'shards','tensor'}, use_global_device_ids=true, to_apply=%region_3.0 | all-reduce | flops 2 | bytes 16 | tf_op jit(solution)/shard_map/psum | solution.py:24
  322.0 1.5 fusion.10
  323.5 0.0 all-reduce.12.cloned.1.call-update
  323.6 0.0 all-reduce.14.cloned.1.call-start
  323.6 121.5 %all-reduce.12.cloned.1.call-done = f32[2,256,256]{2,1,0:T(8,128)} async-done(((f32[2,256,256]{2,1,0:T(8,128)}), f32[2,256,256]{2,1,0:T(8,128)}) %all-reduce.12.cloned.1.call-update) | async-done | bytes 524304 | tf_op jit(solution)/shard_map/psum | solution.py:27
  445.1 1.4 fusion.8
  446.6 1.4 fusion.15
  448.0 0.0 all-reduce.14.cloned.1.call-update
  448.0 0.0 all-reduce.16.cloned.1.call-start
  448.0 127.3 %all-reduce.14.cloned.1.call-done = f32[2,256,256]{2,1,0:T(8,128)} async-done(((f32[2,256,256]{2,1,0:T(8,128)}), f32[2,256,256]{2,1,0:T(8,128)}) %all-reduce.14.cloned.1.call-update) | async-done | bytes 524304 | tf_op jit(solution)/shard_map/psum | solution.py:27
  575.3 1.4 fusion.7
  576.7 1.4 fusion.16
  578.1 0.0 all-reduce.16.cloned.1.call-update
  578.1 0.0 all-reduce.18.cloned.1.call-start
  578.2 127.2 %all-reduce.16.cloned.1.call-done = f32[2,256,256]{2,1,0:T(8,128)} async-done(((f32[2,256,256]{2,1,0:T(8,128)}), f32[2,256,256]{2,1,0:T(8,128)}) %all-reduce.16.cloned.1.call-update) | async-done | bytes 524304 | tf_op jit(solution)/shard_map/psum | solution.py:27
  705.4 1.4 fusion.6
  706.8 1.4 fusion.17
  708.3 0.0 all-reduce.18.cloned.1.call-update
  708.3 0.0 all-reduce.20.cloned.1.call-start
  708.3 127.3 %all-reduce.18.cloned.1.call-done = f32[2,256,256]{2,1,0:T(8,128)} async-done(((f32[2,256,256]{2,1,0:T(8,128)}), f32[2,256,256]{2,1,0:T(8,128)}) %all-reduce.18.cloned.1.call-update) | async-done | bytes 524304 | tf_op jit(solution)/shard_map/psum | solution.py:27
  835.6 1.4 fusion.5
  837.0 1.4 fusion.18
  838.4 0.0 all-reduce.20.cloned.1.call-update
  838.4 0.0 all-reduce.22.cloned.1.call-start
  838.5 127.4 %all-reduce.20.cloned.1.call-done = f32[2,256,256]{2,1,0:T(8,128)} async-done(((f32[2,256,256]{2,1,0:T(8,128)}), f32[2,256,256]{2,1,0:T(8,128)}) %all-reduce.20.cloned.1.call-update) | async-done | bytes 524304 | tf_op jit(solution)/shard_map/psum | solution.py:27
  965.9 1.4 fusion.4
  967.3 22.4 %all_gather.6 = f32[2,192,256]{2,0,1:T(2,128)S(1)} all-gather(f32[2,12,256]{2,0,1:T(2,128)S(1)} %copy.19), channel_id=1, replica_groups=mesh['shards'=16,'tensor'=4,'section'=2] {'shards'}, dimensions={1}, use_global_device_ids=true | all-gather | bytes 417792 | tf_op jit(solution)/shard_map/all_gather | solution.py:55
  989.8 0.0 copy-start.1
  989.8 1.4 fusion.19
  991.2 0.0 copy-start.5
  991.2 0.0 all-reduce.22.cloned.1.call-update
  991.2 0.6 copy-done.10
  991.8 0.0 copy-start.6
  991.8 0.0 copy-done.8
  991.8 0.0 copy-done.9
  991.9 0.6 copy-done.7
  992.5 0.0 copy-done.6
  992.5 0.7 divide_subtract_fusion
  993.2 37.8 %all-reduce.22.cloned.1.call-done = f32[2,256,128]{2,1,0:T(8,128)} async-done(((f32[2,256,128]{2,1,0:T(8,128)}), f32[2,256,128]{2,1,0:T(8,128)}) %all-reduce.22.cloned.1.call-update) | async-done | bytes 262160 | tf_op jit(solution)/shard_map/psum | solution.py:60
  1031.0 0.0 copy-done.4
  1031.0 0.0 copy-done.5
  1031.0 1.5 multiply_divide_fusion
  1032.5 12.4 %all_gather.7 = f32[2,256,128]{2,1,0:T(8,128)S(1)} all-gather(f32[2,64,128]{2,1,0:T(8,128)S(1)} %get-tuple-element.17), channel_id=1, replica_groups=mesh['shards'=16,'tensor'=4,'section'=2] {'tensor'}, dimensions={1}, use_global_device_ids=true | all-gather | bytes 327680 | tf_op jit(solution)/shard_map/all_gather | solution.py:75
  1044.9 0.0 copy-done.1
  1044.9 0.0 copy-done.3
  1044.9 1.2 fusion.3
  (10 shorter events, 0.1 us)
Async XLA Ops:
  7.2 1.0 copy-start
  7.2 48.4 %all-reduce.10.cloned.1.call-start = ((), (), s32[]{:S(2)}) async-start(), calls=%async_computation | async-start | bytes 524288 | tf_op jit(solution)/shard_map/psum | solution.py:49
  10.1 45.5 %copy-start.2 = (bf16[2,192,128]{2,1,0:T(8,128)(2,1)S(1)}, bf16[2,192,128]{2,1,0:T(8,128)(2,1)}, u32[]{:S(2)}) copy-start(bf16[2,192,128]{2,1,0:T(8,128)(2,1)} %param.10) | copy-start | bytes 294916
  10.1 134.1 %all-reduce.24.cloned.1.call-start = ((), (), s32[]{:S(2)}) async-start(), calls=%async_computation.7 | async-start | bytes 786432
  57.9 387.2 %all-reduce.12.cloned.1.call-start = ((), (), s32[]{:S(2)}) async-start(), calls=%async_computation.1 | async-start | bytes 1048576 | tf_op jit(solution)/shard_map/psum | solution.py:27
  58.0 0.7 copy-start.11
  323.6 251.7 %all-reduce.14.cloned.1.call-start = ((), (), s32[]{:S(2)}) async-start(), calls=%async_computation.2 | async-start | bytes 1048576 | tf_op jit(solution)/shard_map/psum | solution.py:27
  448.0 257.4 %all-reduce.16.cloned.1.call-start = ((), (), s32[]{:S(2)}) async-start(), calls=%async_computation.3 | async-start | bytes 1048576 | tf_op jit(solution)/shard_map/psum | solution.py:27
  578.1 257.4 %all-reduce.18.cloned.1.call-start = ((), (), s32[]{:S(2)}) async-start(), calls=%async_computation.4 | async-start | bytes 1048576 | tf_op jit(solution)/shard_map/psum | solution.py:27
  708.3 257.6 %all-reduce.20.cloned.1.call-start = ((), (), s32[]{:S(2)}) async-start(), calls=%async_computation.5 | async-start | bytes 1048576 | tf_op jit(solution)/shard_map/psum | solution.py:27
  838.4 192.5 %all-reduce.22.cloned.1.call-start = ((), (), s32[]{:S(2)}) async-start(), calls=%async_computation.6 | async-start | bytes 524288 | tf_op jit(solution)/shard_map/psum | solution.py:60
  989.8 55.1 %copy-start.1 = (f32[2,192,256]{2,1,0:T(8,128)}, f32[2,192,256]{2,1,0:T(8,128)S(1)}, u32[]{:S(2)}) copy-start(f32[2,192,256]{2,1,0:T(8,128)S(1)} %copy.21) | copy-start | bytes 1179652
  991.1 0.7 copy-start.10
  991.1 0.7 copy-start.8
  991.1 0.7 copy-start.9
  991.1 39.8 %copy-start.4 = (f32[2,64,128]{2,1,0:T(8,128)S(1)}, f32[2,64,128]{2,1,0:T(8,128)}, u32[]{:S(2)}) copy-start(f32[2,64,128]{2,1,0:T(8,128)} %param.14) | copy-start | bytes 196612
  991.2 39.8 %copy-start.5 = (f32[2,64,128]{2,1,0:T(8,128)S(1)}, f32[2,64,128]{2,1,0:T(8,128)}, u32[]{:S(2)}) copy-start(f32[2,64,128]{2,1,0:T(8,128)} %param.13) | copy-start | bytes 196612
  991.8 0.7 copy-start.7
  991.8 0.7 copy-start.6
  1032.5 12.4 %copy-start.3 = (bf16[2,192,128]{2,1,0:T(8,128)(2,1)S(1)}, bf16[2,192,128]{2,1,0:T(8,128)(2,1)}, u32[]{:S(2)}) copy-start(bf16[2,192,128]{2,1,0:T(8,128)(2,1)} %param.11) | copy-start | bytes 294916
Sparse Core Ops, SparseCore 0:
  10.9 44.6 all-reduce.9
  59.3 84.8 all-reduce.23
  323.7 121.4 all-reduce.11
  449.7 125.5 all-reduce.13
  579.9 125.5 all-reduce.15
  710.0 125.5 all-reduce.17
  840.3 125.5 all-reduce.19
  991.3 39.6 all-reduce.21
where the time goes:
time: 1050 us
  waiting for transfers between devices  798 us (76%)
  blocking collectives  212 us (20%)
  matrix products  19.9 us (2%)
  between operations  14.9 us (1%)
    psum x5, waiting for transfers between devices, spread_orthogonalize(): lax.psum(jnp.einsum('mdr,mds->mrs', current, current, precision=precision...  631 us
    psum x1, blocking collectives, spread_orthogonalize(): lax.psum(jnp.sum(ranged * ranged, axis=(1, 2)), ('shards', 'tensor'))  177 us
    unnamed x9, waiting for transfers between devices  84.5 us
    psum x1, waiting for transfers between devices, shards(): lax.psum(jnp.einsum('mdf,mdr->mfr', gradient_widened, projector, precisio...  45.4 us
    psum x1, waiting for transfers between devices, shards(): complete_rows = lax.psum(projected_slice, 'tensor')  37.8 us
    all_gather x1, blocking collectives, shards(): lax.all_gather(spread_orthogonalize(ranged), 'shards', axis=1, tiled=True)  22.4 us
  transfers between devices with their start and end apart: 8, of which 8 were waited for; matrix products, arithmetic and copies ran while one was open for 0% of the time, Pallas kernels for 0%

commit v1 on v0

--- a/solution.py
+++ b/solution.py
@@ -1,3 +1,4 @@
+import functools
 import jax
 import jax.numpy as jnp
 from jax import lax
@@ -13,6 +14,14 @@
 WEIGHT_DECAY = 0.1
 
 
+def _set_gates(arr, peer_axis):
+    moved = lax.all_gather(arr, peer_axis)
+    return jnp.sum(moved, axis=0)
+
+
+deliver_series = functools.partial(_set_gates, peer_axis=("shards", "tensor"))
+
+
 def newton_step(current, gram_matrix):
     return 1.5 * current - 0.5 * jnp.einsum(
         "mdr,mrs->mds", current, gram_matrix, precision=lax.Precision.HIGHEST
@@ -24,9 +33,8 @@
     squares = lax.psum(jnp.sum(ranged * ranged, axis=(1, 2)), ("shards", "tensor"))
     current = ranged / (jnp.sqrt(squares) + NORM_EPS)[:, None, None]
     for sweep_index in range(NS_STEPS):
-        gram_matrix = lax.psum(
-            jnp.einsum("mdr,mds->mrs", current, current, precision=precision_highest),
-            ("shards", "tensor"),
+        gram_matrix = deliver_series(
+            jnp.einsum("mdr,mds->mrs", current, current, precision=precision_highest)
         )
         current = newton_step(current, gram_matrix)
     return current

time: 1050 us -> 1270 us (1.21)
  waiting for transfers between devices: 798 us -> 965 us
  other arithmetic: 3.08 us -> 62.7 us
    all_gather x0 -> x5, waiting for transfers between devices: none -> 795 us  [_set_gates(): moved = lax.all_gather(arr, peer_axis)]
    psum x5 -> x0, waiting for transfers between devices: 631 us -> none  [spread_orthogonalize(): lax.psum(jnp.einsum('mdr,mds->mrs', current, current, precision=precision...]
    reduce_sum x0 -> x5, other arithmetic: none -> 59.6 us  [_set_gates(): return jnp.sum(moved, axis=0)]
where the time goes in v1:
time: 1270 us
  waiting for transfers between devices  965 us (76%)
  blocking collectives  213 us (17%)
  other arithmetic  62.7 us (5%)
  between operations  15 us (1%)
  matrix products  14.9 us (1%)
    all_gather x5, waiting for transfers between devices, _set_gates(): moved = lax.all_gather(arr, peer_axis)  795 us
    psum x1, blocking collectives, spread_orthogonalize(): lax.psum(jnp.sum(ranged * ranged, axis=(1, 2)), ('shards', 'tensor'))  177 us
    unnamed x9, waiting for transfers between devices  84.5 us
    reduce_sum x5, other arithmetic, _set_gates(): return jnp.sum(moved, axis=0)  59.6 us
    psum x1, waiting for transfers between devices, shards(): lax.psum(jnp.einsum('mdf,mdr->mfr', gradient_widened, projector, precisio...  45.4 us
    psum x1, waiting for transfers between devices, shards(): complete_rows = lax.psum(projected_slice, 'tensor')  39.7 us
  transfers between devices with their start and end apart: 8, of which 8 were waited for; matrix products, arithmetic and copies ran while one was open for 0% of the time, Pallas kernels for 0%

profile of v1, /device:TPU:0, one launch (start us, length us, event | category | flops | bytes accessed | tf_op | source)
XLA Modules:
  0.0 1273.9 jit_solution(17376283760000438413)
XLA Ops:
  7.2 0.0 copy-start
  7.2 0.0 all-reduce.5.cloned.1.call-start
  7.2 0.9 copy-done
  8.2 1.9 fusion.14
  10.1 0.0 all-reduce.5.cloned.1.call-update
  10.1 0.0 all-reduce.9.cloned.1.call-start
  10.2 45.4 %all-reduce.5.cloned.1.call-done = f32[2,128,256]{2,1,0:T(8,128)} async-done(((f32[2,128,256]{2,1,0:T(8,128)}), f32[2,128,256]{2,1,0:T(8,128)}) %all-reduce.5.cloned.1.call-update) | async-done | bytes 262160 | tf_op jit(solution)/shard_map/psum | solution.py:57
  55.6 1.3 convolution_bitcast_fusion
  56.9 1.1 copy.17
  57.9 0.0 all-reduce.9.cloned.1.call-update
  57.9 0.0 all-gather.11.cloned.1.call-start
  58.0 1.2 dynamic-slice
  59.9 84.4 %all-reduce.9.cloned.1.call-done = f32[2,192,256]{2,0,1:T(2,128)} async-done(((f32[2,192,256]{2,0,1:T(2,128)}), f32[2,192,256]{2,0,1:T(2,128)}) %all-reduce.9.cloned.1.call-update) | async-done | bytes 393232
  144.2 0.9 multiply_reduce_fusion
  145.1 176.9 %psum.22 = f32[2]{0:T(128)S(1)} all-reduce(f32[2]{0:T(128)S(1)} %get-tuple-element.20), channel_id=1, replica_groups=mesh['shards'=16,'tensor'=4,'section'=2] {'shards','tensor'}, use_global_device_ids=true, to_apply=%region_3.0 | all-reduce | flops 2 | bytes 16 | tf_op jit(solution)/shard_map/psum | solution.py:33
  322.0 1.5 fusion.10
  323.6 0.0 all-gather.11.cloned.1.call-update
  323.6 0.0 all-gather.13.cloned.1.call-start
  323.6 154.0 %all-gather.11.cloned.1.call-done = f32[128,256,256]{2,1,0:T(8,128)} async-done(((f32[2,256,256]{2,1,0:T(8,128)}), f32[128,256,256]{2,1,0:T(8,128)}) %all-gather.11.cloned.1.call-update) | async-done | bytes 33554448 | tf_op jit(solution)/shard_map/all_gather | solution.py:18
  477.7 11.9 reduce_sum.55
  489.6 0.4 fusion.8
  490.0 1.4 fusion.15
  491.4 0.0 all-gather.13.cloned.1.call-update
  491.4 0.0 all-gather.15.cloned.1.call-start
  491.5 160.3 %all-gather.13.cloned.1.call-done = f32[128,256,256]{2,1,0:T(8,128)} async-done(((f32[2,256,256]{2,1,0:T(8,128)}), f32[128,256,256]{2,1,0:T(8,128)}) %all-gather.13.cloned.1.call-update) | async-done | bytes 33554448 | tf_op jit(solution)/shard_map/all_gather | solution.py:18
  651.7 11.9 reduce_sum.56
  663.6 0.4 fusion.7
  664.0 1.5 fusion.16
  665.5 0.0 all-gather.15.cloned.1.call-update
  665.5 0.0 all-gather.17.cloned.1.call-start
  665.5 160.2 %all-gather.15.cloned.1.call-done = f32[128,256,256]{2,1,0:T(8,128)} async-done(((f32[2,256,256]{2,1,0:T(8,128)}), f32[128,256,256]{2,1,0:T(8,128)}) %all-gather.15.cloned.1.call-update) | async-done | bytes 33554448 | tf_op jit(solution)/shard_map/all_gather | solution.py:18
  825.8 11.9 reduce_sum.57
  837.7 0.4 fusion.6
  838.0 1.5 fusion.17
  839.5 0.0 all-gather.17.cloned.1.call-update
  839.5 0.0 all-gather.19.cloned.1.call-start
  839.6 160.2 %all-gather.17.cloned.1.call-done = f32[128,256,256]{2,1,0:T(8,128)} async-done(((f32[2,256,256]{2,1,0:T(8,128)}), f32[128,256,256]{2,1,0:T(8,128)}) %all-gather.17.cloned.1.call-update) | async-done | bytes 33554448 | tf_op jit(solution)/shard_map/all_gather | solution.py:18
  999.8 0.0 copy-start.9
  999.8 0.0 copy-start.10
  999.9 0.0 copy-start.5
  999.9 0.0 copy-start.6
  999.9 0.0 copy-start.4
  999.9 12.0 reduce_sum.58
  1011.9 0.4 fusion.5
  1012.3 1.5 fusion.18
  1013.7 0.0 all-gather.19.cloned.1.call-update
  1013.8 0.0 all-reduce.7.cloned.1.call-start
  1013.8 160.2 %all-gather.19.cloned.1.call-done = f32[128,256,256]{2,1,0:T(8,128)} async-done(((f32[2,256,256]{2,1,0:T(8,128)}), f32[128,256,256]{2,1,0:T(8,128)}) %all-gather.19.cloned.1.call-update) | async-done | bytes 33554448 | tf_op jit(solution)/shard_map/all_gather | solution.py:18
  1174.1 11.9 reduce_sum.59
  1186.0 0.4 fusion.4
  1186.4 23.9 %all_gather.46 = f32[2,192,256]{2,0,1:T(2,128)S(1)} all-gather(f32[2,12,256]{2,0,1:T(2,128)S(1)} %copy.19), channel_id=1, replica_groups=mesh['shards'=16,'tensor'=4,'section'=2] {'shards'}, dimensions={1}, use_global_device_ids=true | all-gather | bytes 417792 | tf_op jit(solution)/shard_map/all_gather | solution.py:63
  1210.3 0.0 copy-done.3
  1210.3 0.0 copy-start.2
  1210.3 1.4 fusion.19
  1211.6 0.0 all-reduce.7.cloned.1.call-update
  1211.7 0.0 copy-done.11
  1211.7 0.0 copy-done.7
  1211.7 0.7 divide_subtract_fusion
  1212.4 39.7 %all-reduce.7.cloned.1.call-done = f32[2,256,128]{2,1,0:T(8,128)} async-done(((f32[2,256,128]{2,1,0:T(8,128)}), f32[2,256,128]{2,1,0:T(8,128)}) %all-reduce.7.cloned.1.call-update) | async-done | bytes 262160 | tf_op jit(solution)/shard_map/psum | solution.py:68
  1252.1 0.0 copy-done.6
  1252.1 1.5 multiply_divide_fusion
  1253.7 12.2 all_gather.47
  1265.9 1.2 fusion.3
  1267.1 0.0 copy-done.1
  (15 shorter events, 0.1 us)
Async XLA Ops:
  7.2 1.0 copy-start
  7.2 48.4 %all-reduce.5.cloned.1.call-start = ((), (), s32[]{:S(2)}) async-start(), calls=%async_computation | async-start | bytes 524288 | tf_op jit(solution)/shard_map/psum | solution.py:57
  10.1 134.1 %all-reduce.9.cloned.1.call-start = ((), (), s32[]{:S(2)}) async-start(), calls=%async_computation.7 | async-start | bytes 786432
  57.9 419.7 %all-gather.11.cloned.1.call-start = ((), (), s32[]{:S(2)}) async-start(), calls=%async_computation.2 | async-start | bytes 34078720 | tf_op jit(solution)/shard_map/all_gather | solution.py:18
  323.6 328.1 %all-gather.13.cloned.1.call-start = ((), (), s32[]{:S(2)}) async-start(), calls=%async_computation.3 | async-start | bytes 34078720 | tf_op jit(solution)/shard_map/all_gather | solution.py:18
  491.4 334.4 %all-gather.15.cloned.1.call-start = ((), (), s32[]{:S(2)}) async-start(), calls=%async_computation.4 | async-start | bytes 34078720 | tf_op jit(solution)/shard_map/all_gather | solution.py:18
  665.5 334.3 %all-gather.17.cloned.1.call-start = ((), (), s32[]{:S(2)}) async-start(), calls=%async_computation.5 | async-start | bytes 34078720 | tf_op jit(solution)/shard_map/all_gather | solution.py:18
  839.5 334.5 %all-gather.19.cloned.1.call-start = ((), (), s32[]{:S(2)}) async-start(), calls=%async_computation.6 | async-start | bytes 34078720 | tf_op jit(solution)/shard_map/all_gather | solution.py:18
  999.8 267.2 %copy-start.1 = (f32[2,192,256]{2,1,0:T(8,128)S(1)}, f32[2,192,256]{2,1,0:T(8,128)}, u32[]{:S(2)}) copy-start(f32[2,192,256]{2,1,0:T(8,128)} %param.12) | copy-start | bytes 1179652
  999.8 210.4 %copy-start.3 = (bf16[2,192,128]{2,1,0:T(8,128)(2,1)S(1)}, bf16[2,192,128]{2,1,0:T(8,128)(2,1)}, u32[]{:S(2)}) copy-start(bf16[2,192,128]{2,1,0:T(8,128)(2,1)} %param.10) | copy-start | bytes 294916
  999.8 211.8 %copy-start.11 = (s32[2]{0:T(128)S(1)}, s32[2]{0:T(128)}, u32[]{:S(2)}) copy-start(s32[2]{0:T(128)} %param.15) | copy-start | bytes 28
  999.8 211.9 %copy-start.7 = (f32[2,192]{1,0:T(2,128)S(1)}, f32[2,192]{1,0:T(2,128)}, u32[]{:S(2)}) copy-start(f32[2,192]{1,0:T(2,128)} %param.16) | copy-start | bytes 4612
  999.8 211.9 %copy-start.8 = (f32[2,192]{1,0:T(2,128)S(1)}, f32[2,192]{1,0:T(2,128)}, u32[]{:S(2)}) copy-start(f32[2,192]{1,0:T(2,128)} %param.17) | copy-start | bytes 4612
  999.8 211.9 %copy-start.9 = (f32[2,192]{1,0:T(2,128)S(1)}, f32[2,192]{1,0:T(2,128)}, u32[]{:S(2)}) copy-start(f32[2,192]{1,0:T(2,128)} %param.18) | copy-start | bytes 4612
  999.8 211.9 %copy-start.10 = (f32[2,192]{1,0:T(2,128)S(1)}, f32[2,192]{1,0:T(2,128)}, u32[]{:S(2)}) copy-start(f32[2,192]{1,0:T(2,128)} %param.19) | copy-start | bytes 4612
  999.9 252.3 %copy-start.5 = (f32[2,64,128]{2,1,0:T(8,128)S(1)}, f32[2,64,128]{2,1,0:T(8,128)}, u32[]{:S(2)}) copy-start(f32[2,64,128]{2,1,0:T(8,128)} %param.14) | copy-start | bytes 196612
  999.9 252.3 %copy-start.6 = (f32[2,64,128]{2,1,0:T(8,128)S(1)}, f32[2,64,128]{2,1,0:T(8,128)}, u32[]{:S(2)}) copy-start(f32[2,64,128]{2,1,0:T(8,128)} %param.13) | copy-start | bytes 196612
  999.9 266.0 %copy-start.4 = (bf16[2,192,128]{2,1,0:T(8,128)(2,1)S(1)}, bf16[2,192,128]{2,1,0:T(8,128)(2,1)}, u32[]{:S(2)}) copy-start(bf16[2,192,128]{2,1,0:T(8,128)(2,1)} %param.11) | copy-start | bytes 294916
  1013.8 238.4 %all-reduce.7.cloned.1.call-start = ((), (), s32[]{:S(2)}) async-start(), calls=%async_computation.1 | async-start | bytes 524288 | tf_op jit(solution)/shard_map/psum | solution.py:68
  1210.3 56.8 %copy-start.2 = (f32[2,192,256]{2,1,0:T(8,128)}, f32[2,192,256]{2,1,0:T(8,128)S(1)}, u32[]{:S(2)}) copy-start(f32[2,192,256]{2,1,0:T(8,128)S(1)} %copy.21) | copy-start | bytes 1179652
Sparse Core Ops, SparseCore 0:
  10.9 44.6 all-reduce.4
  59.3 84.8 all-reduce.8
  323.7 153.9 all-gather.10
  491.5 160.1 all-gather.12
  665.6 160.1 all-gather.14
  839.6 160.1 all-gather.16
  1013.9 160.1 all-gather.18
  1211.8 40.2 all-reduce.6
